TPU v7x, 512 devices: a whole 4x8x8 slice. The times are simulated.
512 devices in a mesh: sims: 32 (over z_lo, y, core), sites: 16 (over x, z_hi).
Axes of the slice: x: 4, y: 8, z: 8 (z_hi: 4, z_lo: 2; z = z_hi * 2 + z_lo), core: 2. Of those that a mesh axis runs over, the one named last changes fastest.
Arguments:
- genotypes: int32 [32, 64, 8192], P('sims', None, 'sites'), may hold values from 0 to 1
- key_prior: bfloat16 [32, 2048], P('sims', 'sites'), may hold values from -300 to 300
- band_reach: int32 [32], P('sims'), may hold values from 128 to 512, as said below
- cotangent: bfloat16 [32, 2048, 512], P('sims', 'sites'), may hold values from -0.09375 to 0.09375
- conv_weight: float32 [4, 64], replicated, may hold values from -3 to 3
- conv_bias: float32 [64], replicated, may hold values from -3 to 3
- mix_weight: float32 [3, 64, 64], replicated, may hold values from -0.4375 to 0.4375
- embed_weight: float32 [64, 512], replicated, may hold values from -0.75 to 0.75
- norm_gain: float32 [512], replicated, may hold values from 0.5 to 1.5
- attn_weight: bfloat16 [4, 512, 512], replicated, may hold values from -0.25 to 0.25
Outputs:
- grad_attention: float32 [1048576], P(('sims', 'sites'))
- grad_conv: float32 [4, 64], replicated
- grad_bias: float32 [64], replicated
- grad_mix: float32 [3, 64, 64], replicated
- grad_embed: float32 [64, 512], replicated
- grad_gain: float32 [512], replicated
Inputs may be any that keep to these rules, and one draw needn't show every extreme that they name: `band_reach`: some evolution has reach exactly 512 in every draw.
All inputs are finite; a program needn't handle non-finite values.
Results may differ from a plain program's by a relative error of at most 0.017.
Values may be sent and summed in bfloat16 or wider, within the bound.
A program may use at most 64 MiB of HBM per device.

v0:
```python
import jax
import jax.numpy as jnp
from jax import lax
from jax.sharding import PartitionSpec as P

HEADS = 8
HEAD_DIM = 64
BAND = 512
HIGH = lax.Precision.HIGHEST
EPS = 1e-06


def extended(cells, sides, width):
    for axis, dim in sides:
        count = lax.axis_size(axis)
        head = lax.slice_in_dim(cells, 0, width, axis=dim)
        tail = lax.slice_in_dim(cells, cells.shape[dim] - width, cells.shape[dim], axis=dim)
        cells = jnp.concatenate(
            [
                lax.ppermute(tail, axis, [(i, (i + 1) % count) for i in range(count)]),
                cells,
                lax.ppermute(head, axis, [((i + 1) % count, i) for i in range(count)]),
            ],
            axis=dim,
        )
    return cells


def from_behind(value, axis, steps):
    count = lax.axis_size(axis)
    pairs = [(source, (source + steps) % count) for source in range(count)]
    return lax.ppermute(value, axis, pairs)


def silu_slope(value):
    sigma = jax.nn.sigmoid(value)
    return sigma * (1.0 + value * (1.0 - sigma))


def block_offsets(count, reach_blocks):
    chosen = []
    taken = []
    for distance in range(reach_blocks + 1):
        for offset in (distance, -distance):
            if offset % count not in taken:
                taken.append(offset % count)
                chosen.append(offset)
    return chosen


def split_heads(array, heads):
    return array.reshape(array.shape[0], array.shape[1], heads, array.shape[2] // heads)


def band_scores(query, keys, prior, query_places, key_places, limit, cycle_tokens, factor):
    scores = jnp.einsum("sqhe,skhe->shqk", query, keys, preferred_element_type=jnp.float32) * factor
    scores = scores + prior.astype(jnp.float32)[:, None, None, :]
    apart = (key_places[None, :] - query_places[:, None]) % cycle_tokens
    apart = jnp.minimum(apart, cycle_tokens - apart)
    inside = apart[None, None] <= limit[:, None, None, None]
    return (scores, inside)


def per_device(
    genotypes,
    key_prior,
    band_reach,
    cotangent,
    conv_weight,
    conv_bias,
    mix_weight,
    embed_weight,
    norm_gain,
    attn_weight,
):
    sims, haps, sites = genotypes.shape
    patch = conv_weight.shape[0]
    local = sites // patch
    width = attn_weight.shape[1]
    heads = HEADS
    factor = HEAD_DIM ** (-0.5)
    count = lax.axis_size("sites")
    cycle_tokens = local * count
    place = lax.axis_index("sites")
    ordinal = jnp.arange(local, dtype=jnp.int32)
    patches = genotypes.astype(jnp.float32).reshape(sims, haps, local, patch)
    pre = (
        jnp.einsum("shtk,kc->shct", patches, conv_weight, precision=HIGH)
        + conv_bias[None, None, :, None]
    )
    pooled = jnp.mean(jax.nn.silu(pre), axis=1)
    pooled_wide = extended(pooled, (("sites", 2),), 1)
    mixed = jnp.zeros((sims, mix_weight.shape[2], local), jnp.float32)
    for shift_by in (-1, 0, 1):
        mixed = mixed + jnp.einsum(
            "co,sct->sot",
            mix_weight[shift_by + 1],
            pooled_wide[:, :, 1 + shift_by : 1 + shift_by + local],
            precision=HIGH,
        )
    activated = jax.nn.silu(mixed)
    embedded = jnp.einsum("sct,cd->std", activated, embed_weight, precision=HIGH).astype(
        jnp.bfloat16
    )
    wide = embedded.astype(jnp.float32)
    inverse = lax.rsqrt(jnp.mean(wide * wide, axis=2, keepdims=True) + EPS)
    normed = (wide * inverse * norm_gain).astype(jnp.bfloat16)
    query = jnp.einsum(
        "std,de->ste", normed, attn_weight[0], preferred_element_type=jnp.float32
    ).astype(jnp.bfloat16)
    keys = jnp.einsum(
        "std,de->ste", normed, attn_weight[1], preferred_element_type=jnp.float32
    ).astype(jnp.bfloat16)
    values = jnp.einsum(
        "std,de->ste", normed, attn_weight[2], preferred_element_type=jnp.float32
    ).astype(jnp.bfloat16)
    query_heads = split_heads(query, heads)
    key_heads = split_heads(keys, heads)
    value_heads = split_heads(values, heads)
    reach_blocks = -(-BAND // local)
    offsets = block_offsets(count, reach_blocks)
    packed = jnp.concatenate([keys, values, key_prior[:, :, None]], axis=2)
    gathered = {0: packed}
    for offset in offsets[1:]:
        gathered[offset] = from_behind(packed, "sites", -offset)
    packed_cat = jnp.concatenate([gathered[offset] for offset in offsets], axis=1)
    key_cat = split_heads(packed_cat[:, :, :width], heads)
    value_cat = split_heads(packed_cat[:, :, width : 2 * width], heads)
    prior_cat = packed_cat[:, :, 2 * width]
    key_places = jnp.concatenate([(place + offset) % count * local + ordinal for offset in offsets])
    query_places = place * local + ordinal
    scores, inside = band_scores(
        query_heads, key_cat, prior_cat, query_places, key_places, band_reach, cycle_tokens, factor
    )
    row_top = jnp.max(jnp.where(inside, scores, -jnp.inf), axis=-1, keepdims=True)
    lifted = jnp.where(inside, jnp.exp(scores - row_top), 0.0)
    row_total = jnp.sum(lifted, axis=-1, keepdims=True)
    prob = lifted / row_total
    prob_half = prob.astype(jnp.bfloat16)
    attended_full = jnp.einsum(
        "shqk,skhe->sqhe", prob_half, value_cat, preferred_element_type=jnp.float32
    )
    attended = attended_full.astype(jnp.bfloat16).reshape(sims, local, width)
    grad_attended = jnp.einsum(
        "std,ed->ste", cotangent, attn_weight[3], preferred_element_type=jnp.float32
    ).astype(jnp.bfloat16)
    grad_heads = split_heads(grad_attended, heads)
    delta = jnp.einsum("sqhe,sqhe->shq", grad_heads.astype(jnp.float32), attended_full)
    grad_prob = jnp.einsum(
        "sqhe,skhe->shqk", grad_heads, value_cat, preferred_element_type=jnp.float32
    )
    grad_scores = (prob * (grad_prob - delta[..., None]) * factor).astype(jnp.bfloat16)
    grad_query = jnp.einsum(
        "shqk,skhe->sqhe", grad_scores, key_cat, preferred_element_type=jnp.float32
    ).astype(jnp.bfloat16)
    grad_query = grad_query.reshape(sims, local, width)
    key_part = jnp.einsum(
        "shqk,sqhe->skhe", grad_scores, query_heads, preferred_element_type=jnp.float32
    )
    value_part = jnp.einsum(
        "shqk,sqhe->skhe", prob_half, grad_heads, preferred_element_type=jnp.float32
    )
    key_sum = key_part[:, 0:local]
    value_sum = value_part[:, 0:local]
    for position, offset in enumerate(offsets[1:], start=1):
        lower = position * local
        both = jnp.concatenate(
            [key_part[:, lower : lower + local], value_part[:, lower : lower + local]], axis=2
        ).astype(jnp.bfloat16)
        back = from_behind(both, "sites", offset).astype(jnp.float32)
        key_sum = key_sum + back[:, :, :heads]
        value_sum = value_sum + back[:, :, heads:]
    grad_keys = key_sum.astype(jnp.bfloat16).reshape(sims, local, width)
    grad_values = value_sum.astype(jnp.bfloat16).reshape(sims, local, width)
    term_query = jnp.einsum("std,ste->de", normed, grad_query, preferred_element_type=jnp.float32)
    term_keys = jnp.einsum("std,ste->de", normed, grad_keys, preferred_element_type=jnp.float32)
    term_values = jnp.einsum("std,ste->de", normed, grad_values, preferred_element_type=jnp.float32)
    term_output = jnp.einsum("std,ste->de", attended, cotangent, preferred_element_type=jnp.float32)
    flat_terms = jnp.stack([term_query, term_keys, term_values, term_output]).reshape(-1)
    grad_attention = lax.psum_scatter(
        lax.psum_scatter(flat_terms, "sims", scatter_dimension=0, tiled=True),
        "sites",
        scatter_dimension=0,
        tiled=True,
    )
    grad_normed = jnp.einsum(
        "ste,de->std", grad_query, attn_weight[0], preferred_element_type=jnp.float32
    )
    grad_normed = grad_normed + jnp.einsum(
        "ste,de->std", grad_keys, attn_weight[1], preferred_element_type=jnp.float32
    )
    grad_normed = grad_normed + jnp.einsum(
        "ste,de->std", grad_values, attn_weight[2], preferred_element_type=jnp.float32
    )
    term_gain = jnp.sum(grad_normed * wide * inverse, axis=(0, 1))
    scaled = grad_normed * norm_gain
    grad_embedded = (
        inverse * scaled - wide * inverse**3 * jnp.sum(scaled * wide, axis=2, keepdims=True) / width
    )
    grad_embedded = grad_embedded + cotangent.astype(jnp.float32)
    term_embed = jnp.einsum("sct,std->cd", activated, grad_embedded, precision=HIGH)
    grad_mixed = jnp.einsum(
        "std,od->sot", grad_embedded, embed_weight, precision=HIGH
    ) * silu_slope(mixed)
    mixed_wide = extended(grad_mixed.astype(jnp.bfloat16), (("sites", 2),), 1).astype(
        grad_mixed.dtype
    )
    mix_terms = []
    grad_pooled = jnp.zeros(pooled.shape, jnp.float32)
    for shift_by in (-1, 0, 1):
        mix_terms.append(
            jnp.einsum(
                "sct,sot->co",
                pooled_wide[:, :, 1 + shift_by : 1 + shift_by + local],
                grad_mixed,
                precision=HIGH,
            )
        )
        grad_pooled = grad_pooled + jnp.einsum(
            "co,sot->sct",
            mix_weight[shift_by + 1],
            mixed_wide[:, :, 1 - shift_by : 1 - shift_by + local],
            precision=HIGH,
        )
    grad_pre = (grad_pooled / haps)[:, None] * silu_slope(pre)
    term_conv = jnp.einsum("shtk,shct->kc", patches, grad_pre, precision=HIGH)
    term_bias = jnp.sum(grad_pre, axis=(0, 1, 3))
    small = (term_conv, term_bias, jnp.stack(mix_terms), term_embed, term_gain)
    flat_small = lax.psum(jnp.concatenate([t.reshape(-1) for t in small]), ("sims", "sites"))
    pieces = []
    lower = 0
    for t in small:
        pieces.append(flat_small[lower : lower + t.size].reshape(t.shape))
        lower += t.size
    grad_conv, grad_bias, grad_mix, grad_embed, grad_gain = pieces
    return (grad_attention, grad_conv, grad_bias, grad_mix, grad_embed, grad_gain)


def solution(mesh):
    placed = (
        P("sims", None, "sites"),
        P("sims", "sites"),
        P("sims"),
        P("sims", "sites", None),
        P(),
        P(),
        P(),
        P(),
        P(),
        P(),
    )
    return jax.shard_map(
        per_device,
        mesh=mesh,
        in_specs=placed,
        out_specs=(P(("sims", "sites")), P(), P(), P(), P(), P()),
        check_vma=False,
    )
```

profile of v0, /device:TPU:8, one launch (start us, length us, event | category | flops | bytes accessed | tf_op | source)
XLA Modules:
  0.0 869.0 jit_solution(17943417780981665908)
XLA Ops:
  8.5 4.5 fusion.16
  13.1 13.1 %collective-permute-start.1 = (f32[1,64,1]{2,1,0:T(8,128)S(1)}, f32[1,64,1]{2,1,0:T(8,128)S(1)}, u32[]{:S(2)}, u32[]{:S(2)}) collective-permute-start(f32[1,64,1]{2,1,0:T(8,128)S(1)} %get-tuple-element.31), channel_id=1, source_target_pairs={{1,0},{2,1},{3,2},{4,3},{5,4},{6,5},{7,6},{8,7},{9,8},{10,9},{11,1... | collective-permute-start | bytes 776 | tf_op jit(solution)/shard_map/ppermute | solution.py:22
  30.2 6.0 collective-permute-done
  42.0 4.6 collective-permute-start.3
  48.6 7.8 collective-permute-start.5
  58.7 9.6 %collective-permute-done.2 = bf16[1,128,1025]{2,1,0:T(8,128)(2,1)} collective-permute-done((bf16[1,128,1025]{2,1,0:T(8,128)(2,1)}, bf16[1,128,1025]{2,1,0:T(8,128)(2,1)}, u32[]{:S(2)}, u32[]{:S(2)}) %collective-permute-start.2) | collective-permute-done | bytes 262432 | tf_op jit(solution)/shard_map/ppermute | solution.py:32
  71.9 2.8 collective-permute-start.8
  76.4 3.8 collective-permute-done.4
  80.3 15.8 %collective-permute-start.9 = (bf16[1,128,1025]{2,1,0:T(8,128)(2,1)}, bf16[1,128,1025]{2,1,0:T(8,128)(2,1)S(1)}, u32[]{:S(2)}, u32[]{:S(2)}) collective-permute-start(bf16[1,128,1025]{2,1,0:T(8,128)(2,1)} %get-tuple-element.28), channel_id=1, source_target_pairs={{0,4},{1,5},{2,6},{3,7},{4,8},{5,9},{6,10},{7,11},{8,12},{9,13},{1... | collective-permute-start | bytes 787208 | tf_op jit(solution)/shard_map/ppermute | solution.py:32
  103.6 2.8 fusion.114
  118.3 6.1 collective-permute-start.10
  124.4 4.0 collective-permute-start.11
  128.5 4.2 collective-permute-start.12
  132.7 7.7 collective-permute-start.13
  142.5 6.9 collective-permute-start.15
  151.7 4.8 collective-permute-start.17
  160.4 4.4 collective-permute-done.14
  166.6 3.1 copy.52
  174.2 9.6 %collective-permute-start.19 = (bf16[1,64,1]{2,1,0:T(8,128)(2,1)S(1)}, bf16[1,64,1]{2,1,0:T(8,128)(2,1)S(1)}, u32[]{:S(2)}, u32[]{:S(2)}) collective-permute-start(bf16[1,64,1]{2,1,0:T(8,128)(2,1)S(1)} %get-tuple-element.33), channel_id=1, source_target_pairs={{0,1},{1,2},{2,3},{3,4},{4,5},{5,6},{6,7},{7,8},{8,9},{9,10},{10,1... | collective-permute-start | bytes 392 | tf_op jit(solution)/shard_map/ppermute | solution.py:20
  186.1 4.4 collective-permute-done.18
  190.8 2.4 fusion.30
  197.0 225.5 %all-reduce.8.cloned.1.call-done = f32[1048576]{0:T(1024)} async-done(((f32[1048576]{0:T(1024)}), f32[1048576]{0:T(1024)}) %all-reduce.8.cloned.1.call-update) | async-done | bytes 4194320
  426.0 267.0 %all-reduce.6.cloned.1.call-done = f32[45888]{0:T(1024)} async-done(((f32[45888]{0:T(1024)}), f32[45888]{0:T(1024)}) %all-reduce.6.cloned.1.call-update) | async-done | bytes 183568 | tf_op jit(solution)/shard_map/psum | solution.py:229
  700.2 161.0 %all-reduce.10.cloned.1.call-done = f32[32768]{0:T(1024)} async-done(((f32[32768]{0:T(1024)}), f32[32768]{0:T(1024)}) %all-reduce.10.cloned.1.call-update) | async-done | bytes 131088
  (170 shorter events, 70.3 us)
Async XLA Ops:
  7.2 415.3 %all-reduce.8.cloned.1.call-start = ((), (), s32[]{:S(2)}) async-start(), calls=%async_computation.1 | async-start | bytes 8388608
  8.5 29.6 %copy-start.1 = (bf16[4,512,512]{2,1,0:T(8,128)(2,1)S(1)}, bf16[4,512,512]{2,1,0:T(8,128)(2,1)}, u32[]{:S(2)}) copy-start(bf16[4,512,512]{2,1,0:T(8,128)(2,1)} %param.19) | copy-start | bytes 6291460
  13.1 16.8 %collective-permute-start.1 = (f32[1,64,1]{2,1,0:T(8,128)S(1)}, f32[1,64,1]{2,1,0:T(8,128)S(1)}, u32[]{:S(2)}, u32[]{:S(2)}) collective-permute-start(f32[1,64,1]{2,1,0:T(8,128)S(1)} %get-tuple-element.31), channel_id=1, source_target_pairs={{1,0},{2,1},{3,2},{4,3},{5,4},{6,5},{7,6},{8,7},{9,8},{10,9},{11,1... | collective-permute-start | bytes 776 | tf_op jit(solution)/shard_map/ppermute | solution.py:22
  26.3 10.0 %collective-permute-start = (f32[1,64,1]{2,1,0:T(8,128)S(1)}, f32[1,64,1]{2,1,0:T(8,128)S(1)}, u32[]{:S(2)}, u32[]{:S(2)}) collective-permute-start(f32[1,64,1]{2,1,0:T(8,128)S(1)} %get-tuple-element.30), channel_id=1, source_target_pairs={{0,1},{1,2},{2,3},{3,4},{4,5},{5,6},{6,7},{7,8},{8,9},{9,10},{10,1... | collective-permute-start | bytes 776 | tf_op jit(solution)/shard_map/ppermute | solution.py:20
  39.5 28.8 %collective-permute-start.2 = (bf16[1,128,1025]{2,1,0:T(8,128)(2,1)}, bf16[1,128,1025]{2,1,0:T(8,128)(2,1)}, u32[]{:S(2)}, u32[]{:S(2)}) collective-permute-start(bf16[1,128,1025]{2,1,0:T(8,128)(2,1)} %get-tuple-element.28), channel_id=1, source_target_pairs={{0,15},{1,0},{2,1},{3,2},{4,3},{5,4},{6,5},{7,6},{8,7},{9,8},{10,9... | collective-permute-start | bytes 787208 | tf_op jit(solution)/shard_map/ppermute | solution.py:32
  42.0 29.9 %collective-permute-start.3 = (bf16[1,128,1025]{2,1,0:T(8,128)(2,1)}, bf16[1,128,1025]{2,1,0:T(8,128)(2,1)}, u32[]{:S(2)}, u32[]{:S(2)}) collective-permute-start(bf16[1,128,1025]{2,1,0:T(8,128)(2,1)} %get-tuple-element.28), channel_id=1, source_target_pairs={{0,1},{1,2},{2,3},{3,4},{4,5},{5,6},{6,7},{7,8},{8,9},{9,10},{10,1... | collective-permute-start | bytes 787208 | tf_op jit(solution)/shard_map/ppermute | solution.py:32
  46.7 33.6 %collective-permute-start.4 = (bf16[1,128,1025]{2,1,0:T(8,128)(2,1)}, bf16[1,128,1025]{2,1,0:T(8,128)(2,1)}, u32[]{:S(2)}, u32[]{:S(2)}) collective-permute-start(bf16[1,128,1025]{2,1,0:T(8,128)(2,1)} %get-tuple-element.28), channel_id=1, source_target_pairs={{0,14},{1,15},{2,0},{3,1},{4,2},{5,3},{6,4},{7,5},{8,6},{9,7},{10,... | collective-permute-start | bytes 787208 | tf_op jit(solution)/shard_map/ppermute | solution.py:32
  48.6 49.2 %collective-permute-start.5 = (bf16[1,128,1025]{2,1,0:T(8,128)(2,1)}, bf16[1,128,1025]{2,1,0:T(8,128)(2,1)}, u32[]{:S(2)}, u32[]{:S(2)}) collective-permute-start(bf16[1,128,1025]{2,1,0:T(8,128)(2,1)} %get-tuple-element.28), channel_id=1, source_target_pairs={{0,2},{1,3},{2,4},{3,5},{4,6},{5,7},{6,8},{7,9},{8,10},{9,11},{10,... | collective-permute-start | bytes 787208 | tf_op jit(solution)/shard_map/ppermute | solution.py:32
  56.4 43.0 %collective-permute-start.6 = (bf16[1,128,1025]{2,1,0:T(8,128)(2,1)}, bf16[1,128,1025]{2,1,0:T(8,128)(2,1)}, u32[]{:S(2)}, u32[]{:S(2)}) collective-permute-start(bf16[1,128,1025]{2,1,0:T(8,128)(2,1)} %get-tuple-element.28), channel_id=1, source_target_pairs={{0,13},{1,14},{2,15},{3,0},{4,1},{5,2},{6,3},{7,4},{8,5},{9,6},{10... | collective-permute-start | bytes 787208 | tf_op jit(solution)/shard_map/ppermute | solution.py:32
  68.3 32.9 %collective-permute-start.7 = (bf16[1,128,1025]{2,1,0:T(8,128)(2,1)}, bf16[1,128,1025]{2,1,0:T(8,128)(2,1)S(1)}, u32[]{:S(2)}, u32[]{:S(2)}) collective-permute-start(bf16[1,128,1025]{2,1,0:T(8,128)(2,1)} %get-tuple-element.28), channel_id=1, source_target_pairs={{0,3},{1,4},{2,5},{3,6},{4,7},{5,8},{6,9},{7,10},{8,11},{9,12},{10... | collective-permute-start | bytes 787208 | tf_op jit(solution)/shard_map/ppermute | solution.py:32
  71.9 30.0 %collective-permute-start.8 = (bf16[1,128,1025]{2,1,0:T(8,128)(2,1)}, bf16[1,128,1025]{2,1,0:T(8,128)(2,1)S(1)}, u32[]{:S(2)}, u32[]{:S(2)}) collective-permute-start(bf16[1,128,1025]{2,1,0:T(8,128)(2,1)} %get-tuple-element.28), channel_id=1, source_target_pairs={{0,12},{1,13},{2,14},{3,15},{4,0},{5,1},{6,2},{7,3},{8,4},{9,5},{1... | collective-permute-start | bytes 787208 | tf_op jit(solution)/shard_map/ppermute | solution.py:32
  80.3 22.6 %collective-permute-start.9 = (bf16[1,128,1025]{2,1,0:T(8,128)(2,1)}, bf16[1,128,1025]{2,1,0:T(8,128)(2,1)S(1)}, u32[]{:S(2)}, u32[]{:S(2)}) collective-permute-start(bf16[1,128,1025]{2,1,0:T(8,128)(2,1)} %get-tuple-element.28), channel_id=1, source_target_pairs={{0,4},{1,5},{2,6},{3,7},{4,8},{5,9},{6,10},{7,11},{8,12},{9,13},{1... | collective-permute-start | bytes 787208 | tf_op jit(solution)/shard_map/ppermute | solution.py:32
  118.3 24.1 %collective-permute-start.10 = (bf16[1,128,16,64]{1,3,2,0:T(8,128)(2,1)S(1)}, bf16[1,128,16,64]{1,3,2,0:T(8,128)(2,1)S(1)}, u32[]{:S(2)}, u32[]{:S(2)}) collective-permute-start(bf16[1,128,16,64]{1,3,2,0:T(8,128)(2,1)S(1)} %pad_maximum_fusion.2), channel_id=1, source_target_pairs={{0,1},{1,2},{2,3},{3,4},{4,5},{5,6},{6,7},{7,8},{8,9},{9,10},{10,1... | collective-permute-start | bytes 786440 | tf_op jit(solution)/shard_map/ppermute | solution.py:32
  124.4 25.0 %collective-permute-start.11 = (bf16[1,128,16,64]{1,3,2,0:T(8,128)(2,1)S(1)}, bf16[1,128,16,64]{1,3,2,0:T(8,128)(2,1)S(1)}, u32[]{:S(2)}, u32[]{:S(2)}) collective-permute-start(bf16[1,128,16,64]{1,3,2,0:T(8,128)(2,1)S(1)} %pad_maximum_fusion.3), channel_id=1, source_target_pairs={{0,15},{1,0},{2,1},{3,2},{4,3},{5,4},{6,5},{7,6},{8,7},{9,8},{10,9... | collective-permute-start | bytes 786440 | tf_op jit(solution)/shard_map/ppermute | solution.py:32
  128.5 23.2 %collective-permute-start.12 = (bf16[1,128,16,64]{1,3,2,0:T(8,128)(2,1)S(1)}, bf16[1,128,16,64]{1,3,2,0:T(8,128)(2,1)S(1)}, u32[]{:S(2)}, u32[]{:S(2)}) collective-permute-start(bf16[1,128,16,64]{1,3,2,0:T(8,128)(2,1)S(1)} %pad_maximum_fusion.4), channel_id=1, source_target_pairs={{0,2},{1,3},{2,4},{3,5},{4,6},{5,7},{6,8},{7,9},{8,10},{9,11},{10,... | collective-permute-start | bytes 786440 | tf_op jit(solution)/shard_map/ppermute | solution.py:32
  132.7 27.7 %collective-permute-start.13 = (bf16[1,128,16,64]{1,3,2,0:T(8,128)(2,1)S(1)}, bf16[1,128,16,64]{1,3,2,0:T(8,128)(2,1)S(1)}, u32[]{:S(2)}, u32[]{:S(2)}) collective-permute-start(bf16[1,128,16,64]{1,3,2,0:T(8,128)(2,1)S(1)} %pad_maximum_fusion.5), channel_id=1, source_target_pairs={{0,14},{1,15},{2,0},{3,1},{4,2},{5,3},{6,4},{7,5},{8,6},{9,7},{10,... | collective-permute-start | bytes 786440 | tf_op jit(solution)/shard_map/ppermute | solution.py:32
  140.4 24.4 %collective-permute-start.14 = (bf16[1,128,16,64]{1,3,2,0:T(8,128)(2,1)S(1)}, bf16[1,128,16,64]{1,3,2,0:T(8,128)(2,1)S(1)}, u32[]{:S(2)}, u32[]{:S(2)}) collective-permute-start(bf16[1,128,16,64]{1,3,2,0:T(8,128)(2,1)S(1)} %pad_maximum_fusion.6), channel_id=1, source_target_pairs={{0,3},{1,4},{2,5},{3,6},{4,7},{5,8},{6,9},{7,10},{8,11},{9,12},{10... | collective-permute-start | bytes 786440 | tf_op jit(solution)/shard_map/ppermute | solution.py:32
  142.5 22.4 %collective-permute-start.15 = (bf16[1,128,16,64]{1,3,2,0:T(8,128)(2,1)S(1)}, bf16[1,128,16,64]{1,3,2,0:T(8,128)(2,1)S(1)}, u32[]{:S(2)}, u32[]{:S(2)}) collective-permute-start(bf16[1,128,16,64]{1,3,2,0:T(8,128)(2,1)S(1)} %pad_maximum_fusion.7), channel_id=1, source_target_pairs={{0,13},{1,14},{2,15},{3,0},{4,1},{5,2},{6,3},{7,4},{8,5},{9,6},{10... | collective-permute-start | bytes 786440 | tf_op jit(solution)/shard_map/ppermute | solution.py:32
  149.4 15.5 %collective-permute-start.16 = (bf16[1,128,16,64]{1,3,2,0:T(8,128)(2,1)S(1)}, bf16[1,128,16,64]{1,3,2,0:T(8,128)(2,1)S(1)}, u32[]{:S(2)}, u32[]{:S(2)}) collective-permute-start(bf16[1,128,16,64]{1,3,2,0:T(8,128)(2,1)S(1)} %pad_maximum_fusion.8), channel_id=1, source_target_pairs={{0,4},{1,5},{2,6},{3,7},{4,8},{5,9},{6,10},{7,11},{8,12},{9,13},{1... | collective-permute-start | bytes 786440 | tf_op jit(solution)/shard_map/ppermute | solution.py:32
  151.7 13.2 %collective-permute-start.17 = (bf16[1,128,16,64]{1,3,2,0:T(8,128)(2,1)S(1)}, bf16[1,128,16,64]{1,3,2,0:T(8,128)(2,1)S(1)}, u32[]{:S(2)}, u32[]{:S(2)}) collective-permute-start(bf16[1,128,16,64]{1,3,2,0:T(8,128)(2,1)S(1)} %pad_maximum_fusion.9), channel_id=1, source_target_pairs={{0,12},{1,13},{2,14},{3,15},{4,0},{5,1},{6,2},{7,3},{8,4},{9,5},{1... | collective-permute-start | bytes 786440 | tf_op jit(solution)/shard_map/ppermute | solution.py:32
  169.8 523.3 %all-reduce.6.cloned.1.call-start = ((), (), s32[]{:S(2)}) async-start(), calls=%async_computation | async-start | bytes 368640 | tf_op jit(solution)/shard_map/psum | solution.py:229
  174.2 11.7 %collective-permute-start.19 = (bf16[1,64,1]{2,1,0:T(8,128)(2,1)S(1)}, bf16[1,64,1]{2,1,0:T(8,128)(2,1)S(1)}, u32[]{:S(2)}, u32[]{:S(2)}) collective-permute-start(bf16[1,64,1]{2,1,0:T(8,128)(2,1)S(1)} %get-tuple-element.33), channel_id=1, source_target_pairs={{0,1},{1,2},{2,3},{3,4},{4,5},{5,6},{6,7},{7,8},{8,9},{9,10},{10,1... | collective-permute-start | bytes 392 | tf_op jit(solution)/shard_map/ppermute | solution.py:20
  184.0 6.5 collective-permute-start.18
  195.1 666.1 %all-reduce.10.cloned.1.call-start = ((), (), s32[]{:S(2)}) async-start(), calls=%async_computation.2 | async-start | bytes 262144
  (17 other events, 214.3 us)
Sparse Core Ops, SparseCore 0:
  169.9 252.5 all-reduce.7
  427.5 265.5 all-reduce.5
  696.2 164.9 all-reduce.9
where the time goes:
time: 870 us; the launch traced here: 869 us
  waiting for transfers between devices  684 us (79%)
  starting transfers between devices  104 us (12%)
  local copies, waits for them, and re-layouts  35.6 us (4%)
  matrix products  19.2 us (2%)
  between operations  16.8 us (2%)
  other arithmetic  9.7 us (1%)
    unnamed x5, waiting for transfers between devices  386 us
    psum x1, waiting for transfers between devices, per_device(): lax.psum(jnp.concatenate([t.reshape(-1) for t in small]), ('sims', 'sites'))  267 us
    ppermute x16, starting transfers between devices, from_behind(): return lax.ppermute(value, axis, pairs)  76.7 us
    unnamed x49, local copies, waits for them, and re-layouts  20.3 us
    ppermute x16, waiting for transfers between devices, from_behind(): return lax.ppermute(value, axis, pairs)  20.2 us
  transfers between devices with their start and end apart: 23, of which 10 were waited for; matrix products, arithmetic and copies ran while one was open for 4% of the time, Pallas kernels for 0%

commit v1 on v0

--- a/solution.py
+++ b/solution.py
@@ -226,7 +226,9 @@
     term_conv = jnp.einsum("shtk,shct->kc", patches, grad_pre, precision=HIGH)
     term_bias = jnp.sum(grad_pre, axis=(0, 1, 3))
     small = (term_conv, term_bias, jnp.stack(mix_terms), term_embed, term_gain)
-    flat_small = lax.psum(jnp.concatenate([t.reshape(-1) for t in small]), ("sims", "sites"))
+    flat_small = jax.lax.psum(
+        jax.lax.psum(jnp.concatenate([t.reshape(-1) for t in small]), "sites"), "sims"
+    )
     pieces = []
     lower = 0
     for t in small:

time: 870 us -> 796 us (0.915)
  waiting for transfers between devices: 684 us -> 598 us
    psum x1, waiting for transfers between devices: 267 us -> 171 us  [per_device(): jax.lax.psum(jnp.concatenate([t.reshape(-1) for t in small]), 'sites')]
    unnamed x5, waiting for transfers between devices: 386 us -> 401 us
    unnamed x49 -> x45, local copies, waits for them, and re-layouts: 20.3 us -> 19.3 us
where the time goes in v1:
time: 796 us; the launch traced here: 794 us
  waiting for transfers between devices  598 us (75%)
  starting transfers between devices  108 us (14%)
  local copies, waits for them, and re-layouts  35.8 us (4%)
  matrix products  23.6 us (3%)
  between operations  16.7 us (2%)
  other arithmetic  11.4 us (1%)
    unnamed x5, waiting for transfers between devices  401 us
    psum x1, waiting for transfers between devices, per_device(): jax.lax.psum(jnp.concatenate([t.reshape(-1) for t in small]), 'sites')  171 us
    ppermute x16, starting transfers between devices, from_behind(): return lax.ppermute(value, axis, pairs)  82.9 us
    unnamed x45, local copies, waits for them, and re-layouts  19.3 us
    ppermute x16, waiting for transfers between devices, from_behind(): return lax.ppermute(value, axis, pairs)  18.7 us
    ppermute x2, starting transfers between devices, extended(): lax.ppermute(head, axis, [((i + 1) % count, i) for i in range(count)])  17.8 us
  transfers between devices with their start and end apart: 23, of which 10 were waited for; matrix products, arithmetic and copies ran while one was open for 4% of the time, Pallas kernels for 0%

profile of v1, /device:TPU:8, one launch (start us, length us, event | category | flops | bytes accessed | tf_op | source)
XLA Modules:
  0.0 794.0 jit_solution(5818837977827067071)
XLA Ops:
  9.1 4.5 fusion.16
  13.7 13.1 %collective-permute-start.1 = (f32[1,64,1]{2,1,0:T(8,128)S(1)}, f32[1,64,1]{2,1,0:T(8,128)S(1)}, u32[]{:S(2)}, u32[]{:S(2)}) collective-permute-start(f32[1,64,1]{2,1,0:T(8,128)S(1)} %get-tuple-element.33), channel_id=1, source_target_pairs={{1,0},{2,1},{3,2},{4,3},{5,4},{6,5},{7,6},{8,7},{9,8},{10,9},{11,1... | collective-permute-start | bytes 776 | tf_op jit(solution)/shard_map/ppermute | solution.py:22
  30.8 6.0 collective-permute-done
  41.7 4.6 collective-permute-start.3
  48.3 7.8 collective-permute-start.5
  58.4 6.0 collective-permute-start.7
  66.2 3.6 collective-permute-done.3
  69.7 4.6 collective-permute-start.8
  76.0 3.9 collective-permute-done.4
  79.9 15.8 %collective-permute-start.9 = (bf16[1,128,1025]{2,1,0:T(8,128)(2,1)}, bf16[1,128,1025]{2,1,0:T(8,128)(2,1)S(1)}, u32[]{:S(2)}, u32[]{:S(2)}) collective-permute-start(bf16[1,128,1025]{2,1,0:T(8,128)(2,1)} %get-tuple-element.30), channel_id=1, source_target_pairs={{0,4},{1,5},{2,6},{3,7},{4,8},{5,9},{6,10},{7,11},{8,12},{9,13},{1... | collective-permute-start | bytes 787208 | tf_op jit(solution)/shard_map/ppermute | solution.py:32
  117.7 6.1 collective-permute-start.10
  123.8 4.1 collective-permute-start.11
  128.0 4.2 collective-permute-start.12
  132.2 7.7 collective-permute-start.13
  142.4 6.9 collective-permute-start.15
  151.3 5.1 collective-permute-start.17
  159.9 8.3 %collective-permute-done.14 = bf16[1,128,16,64]{1,3,2,0:T(8,128)(2,1)S(1)} collective-permute-done((bf16[1,128,16,64]{1,3,2,0:T(8,128)(2,1)S(1)}, bf16[1,128,16,64]{1,3,2,0:T(8,128)(2,1)S(1)}, u32[]{:S(2)}, u32[]{:S(2)}) %collective-permute-start.14) | collective-permute-done | bytes 262176 | tf_op jit(solution)/shard_map/ppermute | solution.py:32
  176.4 5.7 collective-permute-start.19
  182.1 4.7 collective-permute-start.18
  192.5 3.1 fusion.30
  198.2 3.1 copy.52
  201.3 171.2 %all-reduce.7.cloned.1.call-done = f32[45888]{0:T(1024)} async-done(((f32[45888]{0:T(1024)}), f32[45888]{0:T(1024)}) %all-reduce.7.cloned.1.call-update) | async-done | bytes 183568 | tf_op jit(solution)/shard_map/psum | solution.py:230
  374.4 236.3 %all-reduce.11.cloned.1.call-done = (f32[1048576]{0:T(1024)}, f32[45888]{0:T(1024)}) async-done(((f32[1048576]{0:T(1024)}, f32[45888]{0:T(1024)}), (f32[1048576]{0:T(1024)}, f32[45888]{0:T(1024)})) %all-reduce.11.cloned.1.call-update) | async-done | bytes 4377872
  621.5 164.7 %all-reduce.9.cloned.1.call-done = f32[32768]{0:T(1024)} async-done(((f32[32768]{0:T(1024)}), f32[32768]{0:T(1024)}) %all-reduce.9.cloned.1.call-update) | async-done | bytes 131088
  (166 shorter events, 76.0 us)
Async XLA Ops:
  7.2 365.3 %all-reduce.7.cloned.1.call-start = ((), (), s32[]{:S(2)}) async-start(), calls=%async_computation | async-start | bytes 368640 | tf_op jit(solution)/shard_map/psum | solution.py:230
  13.7 16.8 %collective-permute-start.1 = (f32[1,64,1]{2,1,0:T(8,128)S(1)}, f32[1,64,1]{2,1,0:T(8,128)S(1)}, u32[]{:S(2)}, u32[]{:S(2)}) collective-permute-start(f32[1,64,1]{2,1,0:T(8,128)S(1)} %get-tuple-element.33), channel_id=1, source_target_pairs={{1,0},{2,1},{3,2},{4,3},{5,4},{6,5},{7,6},{8,7},{9,8},{10,9},{11,1... | collective-permute-start | bytes 776 | tf_op jit(solution)/shard_map/ppermute | solution.py:22
  26.9 10.0 %collective-permute-start = (f32[1,64,1]{2,1,0:T(8,128)S(1)}, f32[1,64,1]{2,1,0:T(8,128)S(1)}, u32[]{:S(2)}, u32[]{:S(2)}) collective-permute-start(f32[1,64,1]{2,1,0:T(8,128)S(1)} %get-tuple-element.32), channel_id=1, source_target_pairs={{0,1},{1,2},{2,3},{3,4},{4,5},{5,6},{6,7},{7,8},{8,9},{9,10},{10,1... | collective-permute-start | bytes 776 | tf_op jit(solution)/shard_map/ppermute | solution.py:20
  39.1 19.3 %collective-permute-start.2 = (bf16[1,128,1025]{2,1,0:T(8,128)(2,1)}, bf16[1,128,1025]{2,1,0:T(8,128)(2,1)}, u32[]{:S(2)}, u32[]{:S(2)}) collective-permute-start(bf16[1,128,1025]{2,1,0:T(8,128)(2,1)} %get-tuple-element.30), channel_id=1, source_target_pairs={{0,15},{1,0},{2,1},{3,2},{4,3},{5,4},{6,5},{7,6},{8,7},{9,8},{10,9... | collective-permute-start | bytes 787208 | tf_op jit(solution)/shard_map/ppermute | solution.py:32
  41.7 28.0 %collective-permute-start.3 = (bf16[1,128,1025]{2,1,0:T(8,128)(2,1)}, bf16[1,128,1025]{2,1,0:T(8,128)(2,1)}, u32[]{:S(2)}, u32[]{:S(2)}) collective-permute-start(bf16[1,128,1025]{2,1,0:T(8,128)(2,1)} %get-tuple-element.30), channel_id=1, source_target_pairs={{0,1},{1,2},{2,3},{3,4},{4,5},{5,6},{6,7},{7,8},{8,9},{9,10},{10,1... | collective-permute-start | bytes 787208 | tf_op jit(solution)/shard_map/ppermute | solution.py:32
  46.3 33.6 %collective-permute-start.4 = (bf16[1,128,1025]{2,1,0:T(8,128)(2,1)}, bf16[1,128,1025]{2,1,0:T(8,128)(2,1)}, u32[]{:S(2)}, u32[]{:S(2)}) collective-permute-start(bf16[1,128,1025]{2,1,0:T(8,128)(2,1)} %get-tuple-element.30), channel_id=1, source_target_pairs={{0,14},{1,15},{2,0},{3,1},{4,2},{5,3},{6,4},{7,5},{8,6},{9,7},{10,... | collective-permute-start | bytes 787208 | tf_op jit(solution)/shard_map/ppermute | solution.py:32
  48.3 49.2 %collective-permute-start.5 = (bf16[1,128,1025]{2,1,0:T(8,128)(2,1)}, bf16[1,128,1025]{2,1,0:T(8,128)(2,1)}, u32[]{:S(2)}, u32[]{:S(2)}) collective-permute-start(bf16[1,128,1025]{2,1,0:T(8,128)(2,1)} %get-tuple-element.30), channel_id=1, source_target_pairs={{0,2},{1,3},{2,4},{3,5},{4,6},{5,7},{6,8},{7,9},{8,10},{9,11},{10,... | collective-permute-start | bytes 787208 | tf_op jit(solution)/shard_map/ppermute | solution.py:32
  56.1 43.0 %collective-permute-start.6 = (bf16[1,128,1025]{2,1,0:T(8,128)(2,1)}, bf16[1,128,1025]{2,1,0:T(8,128)(2,1)}, u32[]{:S(2)}, u32[]{:S(2)}) collective-permute-start(bf16[1,128,1025]{2,1,0:T(8,128)(2,1)} %get-tuple-element.30), channel_id=1, source_target_pairs={{0,13},{1,14},{2,15},{3,0},{4,1},{5,2},{6,3},{7,4},{8,5},{9,6},{10... | collective-permute-start | bytes 787208 | tf_op jit(solution)/shard_map/ppermute | solution.py:32
  58.4 42.4 %collective-permute-start.7 = (bf16[1,128,1025]{2,1,0:T(8,128)(2,1)}, bf16[1,128,1025]{2,1,0:T(8,128)(2,1)S(1)}, u32[]{:S(2)}, u32[]{:S(2)}) collective-permute-start(bf16[1,128,1025]{2,1,0:T(8,128)(2,1)} %get-tuple-element.30), channel_id=1, source_target_pairs={{0,3},{1,4},{2,5},{3,6},{4,7},{5,8},{6,9},{7,10},{8,11},{9,12},{10... | collective-permute-start | bytes 787208 | tf_op jit(solution)/shard_map/ppermute | solution.py:32
  69.7 31.9 %collective-permute-start.8 = (bf16[1,128,1025]{2,1,0:T(8,128)(2,1)}, bf16[1,128,1025]{2,1,0:T(8,128)(2,1)S(1)}, u32[]{:S(2)}, u32[]{:S(2)}) collective-permute-start(bf16[1,128,1025]{2,1,0:T(8,128)(2,1)} %get-tuple-element.30), channel_id=1, source_target_pairs={{0,12},{1,13},{2,14},{3,15},{4,0},{5,1},{6,2},{7,3},{8,4},{9,5},{1... | collective-permute-start | bytes 787208 | tf_op jit(solution)/shard_map/ppermute | solution.py:32
  79.9 22.6 %collective-permute-start.9 = (bf16[1,128,1025]{2,1,0:T(8,128)(2,1)}, bf16[1,128,1025]{2,1,0:T(8,128)(2,1)S(1)}, u32[]{:S(2)}, u32[]{:S(2)}) collective-permute-start(bf16[1,128,1025]{2,1,0:T(8,128)(2,1)} %get-tuple-element.30), channel_id=1, source_target_pairs={{0,4},{1,5},{2,6},{3,7},{4,8},{5,9},{6,10},{7,11},{8,12},{9,13},{1... | collective-permute-start | bytes 787208 | tf_op jit(solution)/shard_map/ppermute | solution.py:32
  117.7 24.7 %collective-permute-start.10 = (bf16[1,128,16,64]{1,3,2,0:T(8,128)(2,1)S(1)}, bf16[1,128,16,64]{1,3,2,0:T(8,128)(2,1)S(1)}, u32[]{:S(2)}, u32[]{:S(2)}) collective-permute-start(bf16[1,128,16,64]{1,3,2,0:T(8,128)(2,1)S(1)} %pad_maximum_fusion.2), channel_id=1, source_target_pairs={{0,1},{1,2},{2,3},{3,4},{4,5},{5,6},{6,7},{7,8},{8,9},{9,10},{10,1... | collective-permute-start | bytes 786440 | tf_op jit(solution)/shard_map/ppermute | solution.py:32
  123.8 32.6 %copy-start.5 = (bf16[1,128,512]{2,1,0:T(8,128)(2,1)S(1)}, bf16[1,128,512]{2,1,0:T(8,128)(2,1)}, u32[]{:S(2)}) copy-start(bf16[1,128,512]{2,1,0:T(8,128)(2,1)} %param.13) | copy-start | bytes 393220
  123.8 25.5 %collective-permute-start.11 = (bf16[1,128,16,64]{1,3,2,0:T(8,128)(2,1)S(1)}, bf16[1,128,16,64]{1,3,2,0:T(8,128)(2,1)S(1)}, u32[]{:S(2)}, u32[]{:S(2)}) collective-permute-start(bf16[1,128,16,64]{1,3,2,0:T(8,128)(2,1)S(1)} %pad_maximum_fusion.3), channel_id=1, source_target_pairs={{0,15},{1,0},{2,1},{3,2},{4,3},{5,4},{6,5},{7,6},{8,7},{9,8},{10,9... | collective-permute-start | bytes 786440 | tf_op jit(solution)/shard_map/ppermute | solution.py:32
  128.0 23.3 %collective-permute-start.12 = (bf16[1,128,16,64]{1,3,2,0:T(8,128)(2,1)S(1)}, bf16[1,128,16,64]{1,3,2,0:T(8,128)(2,1)S(1)}, u32[]{:S(2)}, u32[]{:S(2)}) collective-permute-start(bf16[1,128,16,64]{1,3,2,0:T(8,128)(2,1)S(1)} %pad_maximum_fusion.4), channel_id=1, source_target_pairs={{0,2},{1,3},{2,4},{3,5},{4,6},{5,7},{6,8},{7,9},{8,10},{9,11},{10,... | collective-permute-start | bytes 786440 | tf_op jit(solution)/shard_map/ppermute | solution.py:32
  132.2 27.7 %collective-permute-start.13 = (bf16[1,128,16,64]{1,3,2,0:T(8,128)(2,1)S(1)}, bf16[1,128,16,64]{1,3,2,0:T(8,128)(2,1)S(1)}, u32[]{:S(2)}, u32[]{:S(2)}) collective-permute-start(bf16[1,128,16,64]{1,3,2,0:T(8,128)(2,1)S(1)} %pad_maximum_fusion.5), channel_id=1, source_target_pairs={{0,14},{1,15},{2,0},{3,1},{4,2},{5,3},{6,4},{7,5},{8,6},{9,7},{10,... | collective-permute-start | bytes 786440 | tf_op jit(solution)/shard_map/ppermute | solution.py:32
  139.9 28.3 %collective-permute-start.14 = (bf16[1,128,16,64]{1,3,2,0:T(8,128)(2,1)S(1)}, bf16[1,128,16,64]{1,3,2,0:T(8,128)(2,1)S(1)}, u32[]{:S(2)}, u32[]{:S(2)}) collective-permute-start(bf16[1,128,16,64]{1,3,2,0:T(8,128)(2,1)S(1)} %pad_maximum_fusion.6), channel_id=1, source_target_pairs={{0,3},{1,4},{2,5},{3,6},{4,7},{5,8},{6,9},{7,10},{8,11},{9,12},{10... | collective-permute-start | bytes 786440 | tf_op jit(solution)/shard_map/ppermute | solution.py:32
  142.4 25.9 %collective-permute-start.15 = (bf16[1,128,16,64]{1,3,2,0:T(8,128)(2,1)S(1)}, bf16[1,128,16,64]{1,3,2,0:T(8,128)(2,1)S(1)}, u32[]{:S(2)}, u32[]{:S(2)}) collective-permute-start(bf16[1,128,16,64]{1,3,2,0:T(8,128)(2,1)S(1)} %pad_maximum_fusion.7), channel_id=1, source_target_pairs={{0,13},{1,14},{2,15},{3,0},{4,1},{5,2},{6,3},{7,4},{8,5},{9,6},{10... | collective-permute-start | bytes 786440 | tf_op jit(solution)/shard_map/ppermute | solution.py:32
  149.4 19.0 %collective-permute-start.16 = (bf16[1,128,16,64]{1,3,2,0:T(8,128)(2,1)S(1)}, bf16[1,128,16,64]{1,3,2,0:T(8,128)(2,1)S(1)}, u32[]{:S(2)}, u32[]{:S(2)}) collective-permute-start(bf16[1,128,16,64]{1,3,2,0:T(8,128)(2,1)S(1)} %pad_maximum_fusion.8), channel_id=1, source_target_pairs={{0,4},{1,5},{2,6},{3,7},{4,8},{5,9},{6,10},{7,11},{8,12},{9,13},{1... | collective-permute-start | bytes 786440 | tf_op jit(solution)/shard_map/ppermute | solution.py:32
  151.3 17.1 %collective-permute-start.17 = (bf16[1,128,16,64]{1,3,2,0:T(8,128)(2,1)S(1)}, bf16[1,128,16,64]{1,3,2,0:T(8,128)(2,1)S(1)}, u32[]{:S(2)}, u32[]{:S(2)}) collective-permute-start(bf16[1,128,16,64]{1,3,2,0:T(8,128)(2,1)S(1)} %pad_maximum_fusion.9), channel_id=1, source_target_pairs={{0,12},{1,13},{2,14},{3,15},{4,0},{5,1},{6,2},{7,3},{8,4},{9,5},{1... | collective-permute-start | bytes 786440 | tf_op jit(solution)/shard_map/ppermute | solution.py:32
  176.4 10.4 %collective-permute-start.19 = (bf16[1,64,1]{2,1,0:T(8,128)(2,1)}, bf16[1,64,1]{2,1,0:T(8,128)(2,1)S(1)}, u32[]{:S(2)}, u32[]{:S(2)}) collective-permute-start(bf16[1,64,1]{2,1,0:T(8,128)(2,1)} %get-tuple-element.35), channel_id=1, source_target_pairs={{0,1},{1,2},{2,3},{3,4},{4,5},{5,6},{6,7},{7,8},{8,9},{9,10},{10,1... | collective-permute-start | bytes 392 | tf_op jit(solution)/shard_map/ppermute | solution.py:20
  182.1 6.7 collective-permute-start.18
  196.5 414.3 %all-reduce.11.cloned.1.call-start = ((), (), s32[]{:S(2)}) async-start(), calls=%async_computation.2 | async-start | bytes 8757248
  372.5 413.7 %all-reduce.9.cloned.1.call-start = ((), (), s32[]{:S(2)}) async-start(), calls=%async_computation.1 | async-start | bytes 262144
  (15 other events, 240.1 us)
Sparse Core Ops, SparseCore 0:
  196.6 175.8 all-reduce.6
  375.8 234.9 all-reduce.10
  613.7 172.4 all-reduce.8
